TPU v7x, 256 devices: a whole 4x4x8 slice. The times are simulated.
256 devices in a mesh: rep: 2 (over core), shard: 128 (over x, z, y).
Axes of the slice: x: 4, y: 4, z: 8, core: 2. Of those that a mesh axis runs over, the one named last changes fastest.
Arguments:
- grad: bfloat16 [192, 512, 2048], P(None, 'shard'), may hold values from -6 to 6
- momentum: bfloat16 [192, 512, 2048], P(None, 'shard'), may hold values from -6 to 6
- owners: int32 [2, 128, 2], replicated, may hold values from 0 to 192, as said below
Outputs:
- new_momentum: bfloat16 [192, 512, 2048], P(None, 'shard')
- update: bfloat16 [192, 512, 2048], P(None, 'shard')
Inputs may be any that keep to these rules, and one draw needn't show every extreme that they name: `owners`: no matrix index appears twice. In each device's row of 2 slots the entries naming matrices come before the empty ones (value 192). In every draw some device has all 2 slots filled, and some matrices are named by no slot.
All inputs are finite; a program needn't handle non-finite values.
Results may differ from a plain program's by a relative error of at most 0.013.
Values may be sent and summed in bfloat16 or wider, within the bound.
A program may use at most 128 MiB of HBM per device.

v0:
```python
import math
import jax
import jax.numpy as jnp
from jax import lax
from jax.sharding import PartitionSpec as P

R = 512
C = 2048
ITERS = 3
coef_a = 3.4445
coef_b = -4.775
coef_c = 2.0315
mom_decay = 0.95


def newton_schulz(matrix):
    whole = matrix.astype(jnp.float32)
    norm_value = jnp.sqrt(jnp.sum(whole * whole))
    current = (whole / (norm_value + 1e-07)).astype(jnp.bfloat16)
    scaled = None
    for turn_index in range(ITERS):
        gram = lax.dot_general(
            current, current, (((1,), (1,)), ((), ())), preferred_element_type=jnp.float32
        ).astype(jnp.bfloat16)
        square = jnp.dot(gram, gram, preferred_element_type=jnp.float32)
        mixer = (coef_b * gram.astype(jnp.float32) + coef_c * square).astype(jnp.bfloat16)
        result = coef_a * current.astype(jnp.float32) + jnp.dot(
            mixer, current, preferred_element_type=jnp.float32
        )
        if turn_index + 1 < ITERS:
            current = result.astype(jnp.bfloat16)
        else:
            scaled = (0.2 * math.sqrt(max(R, C)) * result).astype(jnp.bfloat16)
    return scaled


def spread_lists(owners, matrix_count, replicas, shard_count):
    devices = replicas * shard_count
    entries = owners.reshape(-1)
    alive = entries < matrix_count
    ordinal = jnp.cumsum(alive.astype(jnp.int32)) - 1
    per_device = (matrix_count + devices - 1) // devices
    target = jnp.where(alive, ordinal, devices * per_device)
    packed = (
        jnp.full((devices * per_device + 1,), matrix_count, jnp.int32)
        .at[target]
        .set(entries)[: devices * per_device]
    )
    return packed.reshape(per_device, shard_count, replicas).transpose(2, 1, 0)


def place_rows(returned, chosen, matrix_count):
    local_rows = returned.shape[1] // chosen.shape[1]
    pieces = returned.reshape(chosen.shape[0] * chosen.shape[1], local_rows, returned.shape[2])
    target = chosen.reshape(-1)
    empty = jnp.zeros((matrix_count, local_rows, returned.shape[2]), jnp.bfloat16)
    return empty.at[target].set(pieces, mode="drop")


def body(grad, momentum, owners):
    fresh = mom_decay * momentum.astype(jnp.float32) + grad.astype(jnp.float32)
    new_momentum = fresh.astype(jnp.bfloat16)
    nesterov = (grad.astype(jnp.float32) + mom_decay * fresh).astype(jnp.bfloat16)
    matrix_count = grad.shape[0]
    local_rows = grad.shape[1]
    width = grad.shape[2]
    replicas = lax.axis_size("rep")
    shard_count = lax.axis_size("shard")
    my_rep = lax.axis_index("rep")
    table = spread_lists(owners, matrix_count, replicas, shard_count)
    slot_count = table.shape[2]
    mine = lax.dynamic_index_in_dim(table, my_rep, 0, keepdims=False)
    chosen = mine.T
    usable = chosen < matrix_count
    taken = jnp.take(nesterov, jnp.minimum(chosen, matrix_count - 1), axis=0)
    outgoing = jnp.where(usable[:, :, None, None], taken, jnp.zeros_like(taken))
    outgoing = outgoing.reshape(slot_count, shard_count * local_rows, width)
    finished = lax.map(
        newton_schulz, lax.all_to_all(outgoing, "shard", split_axis=1, concat_axis=1, tiled=True)
    )
    returned = lax.all_to_all(finished, "shard", split_axis=1, concat_axis=1, tiled=True)
    both = lax.all_gather(returned, "rep", axis=0, tiled=True)
    every_choice = table.transpose(0, 2, 1).reshape(replicas * slot_count, shard_count)
    update = place_rows(both, every_choice, matrix_count)
    return (new_momentum, update)


def solution(mesh):
    placed = (P(None, "shard", None), P(None, "shard", None), P())
    return jax.shard_map(
        body,
        mesh=mesh,
        in_specs=placed,
        out_specs=(P(None, "shard", None), P(None, "shard", None)),
        check_vma=False,
    )
```

profile of v0, /device:TPU:1, one launch (start us, length us, event | category | flops | bytes accessed | tf_op | source)
XLA Modules:
  0.0 297.5 jit_solution(2510085038544679176)
XLA Ops:
  7.2 0.7 fusion.27
  7.9 0.8 copy.21
  10.1 2.4 scatter_custom_fusion
  13.1 7.1 %fusion = (bf16[192,4,2048]{2,1,0:T(4,128)(2,1)S(1)}, bf16[192,4,2048]{2,1,0:T(4,128)(2,1)}) fusion(bf16[192,4,2048]{2,1,0:T(4,128)(2,1)} %param.3, bf16[192,4,2048]{2,1,0:T(4,128)(2,1)} %param.4), kind=kLoop, calls=%fused_computation.5 | loop fusion | flops 12582912 | bytes 12582912 | tf_op jit(solution)/shard_map/convert_element_type | solution.py:63
  20.2 3.5 %gather_fusion = bf16[128,4,2048]{2,1,0:T(4,128)(2,1)} fusion(bf16[192,4,2048]{2,1,0:T(4,128)(2,1)S(1)} %get-tuple-element.15, s32[1024]{0:T(1024)S(1)} %pad_clamp_fusion), kind=kCustom, calls=%fused_computation | custom fusion | bytes 4194816 | tf_op jit(solution)/shard_map/jit(_take)/gather | solution.py:75
  23.7 2.5 gather.7
  26.7 0.3 select_select_fusion
  27.0 5.2 %copy.32 = bf16[1,512,2048]{2,0,1:T(2,128)(2,1)} copy(bf16[1,512,2048]{2,1,0:T(8,128)(2,1)S(1)} %select_select_fusion) | data formatting | bytes 4194304 | tf_op jit(solution)/shard_map/jit(_where)/select_n | solution.py:76
  32.2 0.5 broadcast.218
  32.7 13.1 %reduce.9 = bf16[512,2048]{1,0:T(8,128)(2,1)S(1)} reduce(bf16[512,1,2048]{2,1,0:T(2,128)(2,1)} %bitcast.34, bf16[]{:T(256)} %broadcast.218), dimensions={1}, to_apply=%bitcast.31.reduce_sub_computation | reduce | bytes 4194306
  45.8 2.8 reshape.240
  48.7 65.8 %all_to_all.10 = bf16[128,2,4096]{2,1,0:T(2,128)(2,1)S(1)} all-to-all(bf16[128,2,4096]{2,1,0:T(2,128)(2,1)} %reshape.240), channel_id=1, replica_groups=mesh['rep'=2,'shard'=128] {'shard'}, dimensions={0} | all-to-all | bytes 4194304 | tf_op jit(solution)/shard_map/all_to_all | solution.py:79
  114.4 6.8 %reshape.241 = bf16[512,1,2048]{2,1,0:T(2,128)(2,1)} reshape(bf16[128,2,4096]{2,1,0:T(2,128)(2,1)S(1)} %all_to_all.10) | data formatting | bytes 4194304
  121.2 4.8 %fusion.2 = f32[]{:T(128)} fusion(bf16[1,512,2048]{2,0,1:T(2,128)(2,1)} %bitcast.32), kind=kLoop, calls=%fused_computation.9 | loop fusion | flops 3145727 | bytes 2097156 | tf_op jit(solution)/shard_map/while/body/eval_jaxpr/reduce_sum | solution.py:18
  126.7 3.8 %fusion.5 = bf16[512,2048]{1,0:T(8,128)(2,1)S(1)} fusion(f32[]{:T(128)S(6)} %add.96, bf16[1,512,2048]{2,0,1:T(2,128)(2,1)} %bitcast.33), kind=kLoop, calls=%fused_computation.15 | loop fusion | flops 3145728 | bytes 4194308 | tf_op jit(solution)/shard_map/while/body/eval_jaxpr/convert_element_type | solution.py:19
  130.5 1.3 convolution_convert_fusion.2
  131.8 2.9 add_convert_fusion.1
  134.7 3.6 %convolution_convert_fusion.1 = bf16[512,512]{1,0:T(8,128)(2,1)S(1)} fusion(bf16[512,2048]{1,0:T(8,128)(2,1)} %add_convert_fusion.1), kind=kOutput, calls=%fused_computation.27 | convolution fusion | flops 1074003968 | bytes 2621440 | tf_op jit(solution)/shard_map/while/body/eval_jaxpr/dot_general | solution.py:22
  138.3 2.9 add_convert_fusion
  141.2 3.5 %convolution_convert_fusion = bf16[512,512]{1,0:T(8,128)(2,1)S(1)} fusion(bf16[512,2048]{1,0:T(8,128)(2,1)} %add_convert_fusion), kind=kOutput, calls=%fused_computation.26 | convolution fusion | flops 1074003968 | bytes 2621440 | tf_op jit(solution)/shard_map/while/body/eval_jaxpr/dot_general | solution.py:22
  144.7 3.8 %fusion.4 = bf16[1,512,2048]{2,1,0:T(8,128)(2,1)S(1)} fusion(bf16[512,2048]{1,0:T(8,128)(2,1)} %add_convert_fusion, bf16[512,512]{1,0:T(8,128)(2,1)S(1)} %convolution_convert_fusion), kind=kOutput, calls=%fused_computation.14 | convolution fusion | flops 1348730880 | bytes 4718592 | tf_op jit(solution)/shard_map/while/body/eval_jaxpr/dot_general | solution.py:27
  148.5 5.4 %copy.31 = bf16[1,512,2048]{2,0,1:T(2,128)(2,1)} copy(bf16[1,512,2048]{2,1,0:T(8,128)(2,1)S(1)} %fusion.4) | data formatting | bytes 4194304 | tf_op jit(solution)/shard_map/while/body/jit(dynamic_update_index_in_dim)/broadcast_in_dim | solution.py:78
  153.9 13.1 %reduce.10 = bf16[512,2048]{1,0:T(8,128)(2,1)S(1)} reduce(bf16[512,1,2048]{2,1,0:T(2,128)(2,1)} %bitcast.35, bf16[]{:T(256)} %broadcast.218), dimensions={1}, to_apply=%bitcast.30.reduce_sub_computation | reduce | bytes 4194306
  167.0 2.8 reshape.242
  169.9 58.7 %all_to_all.11 = bf16[128,2,4096]{2,1,0:T(2,128)(2,1)S(1)} all-to-all(bf16[128,2,4096]{2,1,0:T(2,128)(2,1)} %reshape.242), channel_id=1, replica_groups=mesh['rep'=2,'shard'=128] {'shard'}, dimensions={0} | all-to-all | bytes 4194304 | tf_op jit(solution)/shard_map/all_to_all | solution.py:81
  228.6 6.8 %reshape.243 = bf16[512,1,2048]{2,1,0:T(2,128)(2,1)} reshape(bf16[128,2,4096]{2,1,0:T(2,128)(2,1)S(1)} %all_to_all.11) | data formatting | bytes 4194304
  235.3 4.8 %copy.26 = bf16[1,512,2048]{2,1,0:T(8,128)(2,1)} copy(bf16[1,512,2048]{2,0,1:T(2,128)(2,1)} %bitcast.36) | data formatting | bytes 4194304 | tf_op jit(solution)/shard_map/all_to_all | solution.py:81
  240.2 17.8 %all-gather.2.cloned.1.call-done = bf16[2,512,2048]{2,1,0:T(8,128)(2,1)} async-done(((bf16[1,512,2048]{2,1,0:T(8,128)(2,1)}), bf16[2,512,2048]{2,1,0:T(8,128)(2,1)}) %all-gather.2.cloned.1.call-update) | async-done | bytes 4194320 | tf_op jit(solution)/shard_map/all_gather | solution.py:82
  258.0 7.2 %reshape.229 = bf16[256,4,2048]{2,1,0:T(4,128)(2,1)} reshape(bf16[2,512,2048]{2,1,0:T(8,128)(2,1)} %all-gather.2.cloned.1.call-done) | data formatting | bytes 8388608 | tf_op jit(solution)/shard_map/reshape | solution.py:54
  265.2 1.6 broadcast_in_dim.48
  266.8 22.2 %scatter_fusion = bf16[192,4,2048]{2,1,0:T(4,128)(2,1)S(1)} fusion(bf16[192,4,2048]{2,1,0:T(4,128)(2,1)S(1)} %broadcast_in_dim.48, s32[256]{0:T(256)S(1)} %bitcast.39, bf16[256,4,2048]{2,1,0:T(4,128)(2,1)} %reshape.229), kind=kCustom, calls=%fused_computation.2 | custom fusion | bytes 12583936 | tf_op jit(solution)/shard_map/scatter | solution.py:57
  289.0 1.7 copy-done
  (27 shorter events, 2.4 us)
Async XLA Ops:
  7.2 250.8 %all-gather.2.cloned.1.call-start = ((), (), s32[]{:S(2)}) async-start(), calls=%async_computation.2 | async-start | bytes 6291456 | tf_op jit(solution)/shard_map/all_gather | solution.py:82
  134.6 3.7 %copy-start.1 = (bf16[512,2048]{1,0:T(8,128)(2,1)S(1)}, bf16[512,2048]{1,0:T(8,128)(2,1)}, u32[]{:S(2)}) copy-start(bf16[512,2048]{1,0:T(8,128)(2,1)} %add_convert_fusion.1) | copy-start | bytes 6291460
  289.0 1.7 copy-start
Sparse Core Ops, SparseCore 0:
  240.3 17.6 all-gather.1
where the time goes:
time: 299 us; the launch traced here: 298 us
  blocking collectives  124 us (41%)
  local copies, waits for them, and re-layouts  78.6 us (26%)
  other arithmetic  43.7 us (15%)
  matrix products  18 us (6%)
  waiting for transfers between devices  17.8 us (6%)
  between operations  14.9 us (5%)
    all_to_all x1, blocking collectives, body(): lax.all_to_all(outgoing, 'shard', split_axis=1, concat_axis=1, tiled=True)  65.8 us
    all_to_all x1, blocking collectives, body(): lax.all_to_all(finished, 'shard', split_axis=1, concat_axis=1, tiled=True)  58.7 us
    unnamed x2, other arithmetic  26.2 us
    scatter x1, local copies, waits for them, and re-layouts, place_rows(): return empty.at[target].set(pieces, mode='drop')  22.2 us
    unnamed x10, local copies, waits for them, and re-layouts  22.2 us
    all_gather x1, waiting for transfers between devices, body(): both = lax.all_gather(returned, 'rep', axis=0, tiled=True)  17.8 us
    dot_general x3, matrix products, newton_schulz(): jnp.dot(mixer, current, preferred_element_type=jnp.float32)  9.57 us
    dot_general x3, matrix products, newton_schulz(): lax.dot_general(current, current, (((1,), (1,)), ((), ())), preferred_ele...  8.43 us
  transfers between devices with their start and end apart: 1, of which 1 were waited for; matrix products, arithmetic and copies ran while one was open for 0% of the time, Pallas kernels for 0%

commit v1 on v0

--- a/solution.py
+++ b/solution.py
@@ -78,7 +78,12 @@
     finished = lax.map(
         newton_schulz, lax.all_to_all(outgoing, "shard", split_axis=1, concat_axis=1, tiled=True)
     )
-    returned = lax.all_to_all(finished, "shard", split_axis=1, concat_axis=1, tiled=True)
+    returned = jnp.concatenate(
+        lax.all_to_all(
+            jnp.stack(jnp.split(finished, lax.axis_size("shard"), axis=1)), "shard", 0, 0
+        ),
+        axis=1,
+    )
     both = lax.all_gather(returned, "rep", axis=0, tiled=True)
     every_choice = table.transpose(0, 2, 1).reshape(replicas * slot_count, shard_count)
     update = place_rows(both, every_choice, matrix_count)

time: 299 us -> 271 us (0.906)
  local copies, waits for them, and re-layouts: 78.6 us -> 63.3 us
  other arithmetic: 43.7 us -> 30.7 us
    unnamed x2 -> x1, other arithmetic: 26.2 us -> 13.2 us
    unnamed x10 -> x135, local copies, waits for them, and re-layouts: 22.2 us -> 15 us
    broadcast_in_dim x1 -> x0, local copies, waits for them, and re-layouts: 5.38 us -> none  [body(): lax.map(newton_schulz, lax.all_to_all(outgoing, 'shard', split_axis=1, co...]
    all_to_all x1 -> x0, local copies, waits for them, and re-layouts: 4.78 us -> none  [body(): lax.all_to_all(finished, 'shard', split_axis=1, concat_axis=1, tiled=True)]
where the time goes in v1:
time: 271 us; the launch traced here: 270 us
  blocking collectives  124 us (46%)
  local copies, waits for them, and re-layouts  63.3 us (23%)
  other arithmetic  30.7 us (11%)
  matrix products  18 us (7%)
  waiting for transfers between devices  17.8 us (7%)
  between operations  15.5 us (6%)
    all_to_all x1, blocking collectives, body(): lax.all_to_all(outgoing, 'shard', split_axis=1, concat_axis=1, tiled=True)  65.8 us
    all_to_all x1, blocking collectives, body(): lax.all_to_all(jnp.stack(jnp.split(finished, lax.axis_size('shard'), axis...  58.5 us
    scatter x1, local copies, waits for them, and re-layouts, place_rows(): return empty.at[target].set(pieces, mode='drop')  22.2 us
    all_gather x1, waiting for transfers between devices, body(): both = lax.all_gather(returned, 'rep', axis=0, tiled=True)  17.8 us
    unnamed x135, local copies, waits for them, and re-layouts  15 us
    unnamed x1, other arithmetic  13.2 us
    dot_general x3, matrix products, newton_schulz(): jnp.dot(mixer, current, preferred_element_type=jnp.float32)  9.56 us
    dot_general x3, matrix products, newton_schulz(): lax.dot_general(current, current, (((1,), (1,)), ((), ())), preferred_ele...  8.43 us
  transfers between devices with their start and end apart: 1, of which 1 were waited for; matrix products, arithmetic and copies ran while one was open for 0% of the time, Pallas kernels for 0%

profile of v1, /device:TPU:1, one launch (start us, length us, event | category | flops | bytes accessed | tf_op | source)
XLA Modules:
  0.0 269.5 jit_solution(8175058781972107704)
XLA Ops:
  7.2 0.7 fusion.27
  7.9 0.8 copy.19
  9.0 0.3 reduce-window.9
  9.6 0.2 copy.17
  10.1 2.4 scatter_custom_fusion
  12.9 0.2 compare_reduce_fusion
  13.1 7.1 %fusion = (bf16[192,4,2048]{2,1,0:T(4,128)(2,1)S(1)}, bf16[192,4,2048]{2,1,0:T(4,128)(2,1)}) fusion(bf16[192,4,2048]{2,1,0:T(4,128)(2,1)} %param.3, bf16[192,4,2048]{2,1,0:T(4,128)(2,1)} %param.4), kind=kLoop, calls=%fused_computation.5 | loop fusion | flops 12582912 | bytes 12582912 | tf_op jit(solution)/shard_map/convert_element_type | solution.py:63
  20.2 3.5 %gather_fusion = bf16[128,4,2048]{2,1,0:T(4,128)(2,1)} fusion(bf16[192,4,2048]{2,1,0:T(4,128)(2,1)S(1)} %get-tuple-element.15, s32[1024]{0:T(1024)S(1)} %pad_clamp_fusion), kind=kCustom, calls=%fused_computation | custom fusion | bytes 4194816 | tf_op jit(solution)/shard_map/jit(_take)/gather | solution.py:75
  23.7 2.5 gather.7
  26.7 0.3 select_select_fusion
  27.0 5.2 %copy.26 = bf16[1,512,2048]{2,0,1:T(2,128)(2,1)} copy(bf16[1,512,2048]{2,1,0:T(8,128)(2,1)S(1)} %select_select_fusion) | data formatting | bytes 4194304 | tf_op jit(solution)/shard_map/jit(_where)/select_n | solution.py:76
  32.2 0.5 broadcast.218
  32.7 13.2 %reduce.9 = bf16[512,2048]{1,0:T(8,128)(2,1)S(1)} reduce(bf16[512,1,2048]{2,1,0:T(2,128)(2,1)} %bitcast.542, bf16[]{:T(256)} %broadcast.218), dimensions={1}, to_apply=%bitcast.539.reduce_sub_computation | reduce | bytes 4194306
  45.9 2.8 %reshape.244 = bf16[128,2,4096]{2,1,0:T(2,128)(2,1)} reshape(bf16[512,2048]{1,0:T(8,128)(2,1)S(1)} %reduce.9) | data formatting | bytes 4194304
  48.7 65.8 %all_to_all.10 = bf16[128,2,4096]{2,1,0:T(2,128)(2,1)S(1)} all-to-all(bf16[128,2,4096]{2,1,0:T(2,128)(2,1)} %reshape.244), channel_id=1, replica_groups=mesh['rep'=2,'shard'=128] {'shard'}, dimensions={0} | all-to-all | bytes 4194304 | tf_op jit(solution)/shard_map/all_to_all | solution.py:79
  114.5 6.8 %reshape.245 = bf16[512,1,2048]{2,1,0:T(2,128)(2,1)} reshape(bf16[128,2,4096]{2,1,0:T(2,128)(2,1)S(1)} %all_to_all.10) | data formatting | bytes 4194304
  121.2 4.8 %fusion.2 = f32[]{:T(128)} fusion(bf16[1,512,2048]{2,0,1:T(2,128)(2,1)} %bitcast.540), kind=kLoop, calls=%fused_computation.9 | loop fusion | flops 3145727 | bytes 2097156 | tf_op jit(solution)/shard_map/while/body/eval_jaxpr/reduce_sum | solution.py:18
  126.7 3.8 %fusion.5 = bf16[512,2048]{1,0:T(8,128)(2,1)S(1)} fusion(f32[]{:T(128)S(6)} %add.96, bf16[1,512,2048]{2,0,1:T(2,128)(2,1)} %bitcast.541), kind=kLoop, calls=%fused_computation.15 | loop fusion | flops 3145728 | bytes 4194308 | tf_op jit(solution)/shard_map/while/body/eval_jaxpr/convert_element_type | solution.py:19
  130.5 1.3 convolution_convert_fusion.2
  131.8 2.9 %add_convert_fusion.1 = bf16[512,2048]{1,0:T(8,128)(2,1)} fusion(bf16[512,2048]{1,0:T(8,128)(2,1)S(1)} %fusion.5, bf16[512,512]{1,0:T(8,128)(2,1)S(1)} %convolution_convert_fusion.2), kind=kOutput, calls=%fused_computation.13 | convolution fusion | flops 1347682304 | bytes 4718592 | tf_op jit(solution)/shard_map/while/body/eval_jaxpr/dot_general | solution.py:27
  134.7 3.6 %convolution_convert_fusion.1 = bf16[512,512]{1,0:T(8,128)(2,1)S(1)} fusion(bf16[512,2048]{1,0:T(8,128)(2,1)} %add_convert_fusion.1), kind=kOutput, calls=%fused_computation.27 | convolution fusion | flops 1074003968 | bytes 2621440 | tf_op jit(solution)/shard_map/while/body/eval_jaxpr/dot_general | solution.py:22
  138.3 2.9 %add_convert_fusion = bf16[512,2048]{1,0:T(8,128)(2,1)} fusion(bf16[512,2048]{1,0:T(8,128)(2,1)S(1)} %copy-done.1, bf16[512,512]{1,0:T(8,128)(2,1)S(1)} %convolution_convert_fusion.1), kind=kOutput, calls=%fused_computation.12 | convolution fusion | flops 1347682304 | bytes 4718592 | tf_op jit(solution)/shard_map/while/body/eval_jaxpr/dot_general | solution.py:27
  141.2 3.5 %convolution_convert_fusion = bf16[512,512]{1,0:T(8,128)(2,1)S(1)} fusion(bf16[512,2048]{1,0:T(8,128)(2,1)} %add_convert_fusion), kind=kOutput, calls=%fused_computation.26 | convolution fusion | flops 1074003968 | bytes 2621440 | tf_op jit(solution)/shard_map/while/body/eval_jaxpr/dot_general | solution.py:22
  144.7 3.8 %fusion.4 = bf16[1,512,2048]{2,1,0:T(8,128)(2,1)S(1)} fusion(bf16[512,2048]{1,0:T(8,128)(2,1)} %add_convert_fusion, bf16[512,512]{1,0:T(8,128)(2,1)S(1)} %convolution_convert_fusion), kind=kOutput, calls=%fused_computation.14 | convolution fusion | flops 1348730880 | bytes 4718592 | tf_op jit(solution)/shard_map/while/body/eval_jaxpr/dot_general | solution.py:27
  149.9 0.2 constant_dynamic-update-slice_fusion.67
  151.6 58.5 %all_to_all.11 = bf16[128,1,4,2048]{3,2,1,0:T(4,128)(2,1)S(1)} all-to-all(bf16[128,1,4,2048]{3,2,1,0:T(4,128)(2,1)S(1)} %constant_dynamic-update-slice_fusion), channel_id=1, replica_groups=mesh['rep'=2,'shard'=128] {'shard'}, dimensions={0} | all-to-all | bytes 4194304 | tf_op jit(solution)/shard_map/all_to_all | solution.py:82
  210.1 2.0 reshape.210
  212.2 17.8 %all-gather.2.cloned.1.call-done = bf16[2,512,2048]{2,1,0:T(8,128)(2,1)} async-done(((bf16[1,512,2048]{2,1,0:T(8,128)(2,1)}), bf16[2,512,2048]{2,1,0:T(8,128)(2,1)}) %all-gather.2.cloned.1.call-update) | async-done | bytes 4194320 | tf_op jit(solution)/shard_map/all_gather | solution.py:87
  230.0 7.2 %reshape.233 = bf16[256,4,2048]{2,1,0:T(4,128)(2,1)} reshape(bf16[2,512,2048]{2,1,0:T(8,128)(2,1)} %all-gather.2.cloned.1.call-done) | data formatting | bytes 8388608 | tf_op jit(solution)/shard_map/reshape | solution.py:54
  237.2 1.6 broadcast_in_dim.48
  238.8 22.2 %scatter_fusion = bf16[192,4,2048]{2,1,0:T(4,128)(2,1)S(1)} fusion(bf16[192,4,2048]{2,1,0:T(4,128)(2,1)S(1)} %broadcast_in_dim.48, s32[256]{0:T(256)S(1)} %bitcast.545, bf16[256,4,2048]{2,1,0:T(4,128)(2,1)} %reshape.233), kind=kCustom, calls=%fused_computation.2 | custom fusion | bytes 12583936 | tf_op jit(solution)/shard_map/scatter | solution.py:57
  261.0 1.7 copy-done
  (151 shorter events, 4.0 us)
Async XLA Ops:
  7.2 222.8 %all-gather.2.cloned.1.call-start = ((), (), s32[]{:S(2)}) async-start(), calls=%async_computation.2 | async-start | bytes 6291456 | tf_op jit(solution)/shard_map/all_gather | solution.py:87
  134.7 3.7 %copy-start.1 = (bf16[512,2048]{1,0:T(8,128)(2,1)S(1)}, bf16[512,2048]{1,0:T(8,128)(2,1)}, u32[]{:S(2)}) copy-start(bf16[512,2048]{1,0:T(8,128)(2,1)} %add_convert_fusion.1) | copy-start | bytes 6291460
  261.0 1.7 copy-start
Sparse Core Ops, SparseCore 0:
  212.3 17.6 all-gather.1
